TPU v7x, 32 devices: a whole 2x2x4 slice. The times are simulated.
32 devices in a mesh: replica: 8 (over z, core), shard: 4 (over y, x).
Axes of the slice: x: 2, y: 2, z: 4, core: 2. Of those that a mesh axis runs over, the one named last changes fastest.
Arguments:
- tokens: bfloat16 [32768, 2560], P(('replica', 'shard')), may hold values from -6 to 6
- w_in: bfloat16 [2560, 10496], P('shard'), may hold values from -0.125 to 0.125
- w_dt: bfloat16 [2560, 80], P('shard'), may hold values from -0.125 to 0.125
- w_out: bfloat16 [5120, 2560], P('shard'), may hold values from -0.078125 to 0.078125
- norm_gain: float32 [2560], replicated, may hold values from 0.5 to 1.5
- conv_weight: float32 [4, 5376], replicated, may hold values from -3 to 3
- conv_bias: float32 [5376], replicated, may hold values from -1.5 to 1.5
- dt_bias: float32 [80], replicated, may hold values from -5 to -1
- a_log: float32 [80], replicated, may hold values from -3 to 2.5
- d_skip: float32 [80], replicated, may hold values from 0.5 to 1.5
- gate_gain: float32 [5120], replicated, may hold values from 0.5 to 1.5
- cotangent: bfloat16 [32768, 2560], P(('replica', 'shard')), may hold values from -8 to 8
Outputs:
- result: bfloat16 [32768, 2560], P(('replica', 'shard'))
- token_grad: float32 [32768, 2560], P(('replica', 'shard'))
- grad_w_in: float32 [2560, 10496], P('shard')
- grad_w_dt: float32 [2560, 80], P('shard')
- grad_w_out: float32 [5120, 2560], P('shard')
- grad_norm_gain: float32 [2560], replicated
- grad_conv_weight: float32 [4, 5376], replicated
- grad_conv_bias: float32 [5376], replicated
- grad_dt_bias: float32 [80], replicated
- grad_a_log: float32 [80], replicated
- grad_d_skip: float32 [80], replicated
- grad_gate_gain: float32 [5120], replicated
All inputs are finite; a program needn't handle non-finite values.
Results may differ from a plain program's by a relative error of at most 0.017.
Values may be sent and summed in bfloat16 or wider, within the bound.
No kernel may reach another device: no remote copies, remote signals or barrier semaphores. Data moves between devices by JAX's collectives and lax.ppermute only.
A program may use at most 768 MiB of HBM per device.

v0:
```python
import jax
import jax.numpy as jnp
from jax import lax
from jax.sharding import PartitionSpec as P

H = 80
P_SIZE = 64
E = 5120
NST = 128
CONVK = 4
SPAN = 256


eps = 1e-05


def rms_norm(tokens_f, gain):
    return tokens_f * lax.rsqrt(jnp.mean(tokens_f * tokens_f, axis=-1, keepdims=True) + eps) * gain


def contract_rows(left, right):
    return lax.dot_general(
        left, right, (((0,), (0,)), ((), ())), preferred_element_type=jnp.float32
    )


def contract_cols(left, right):
    return lax.dot_general(
        left, right, (((1,), (1,)), ((), ())), preferred_element_type=jnp.float32
    )


def ssd_scan(values, step_size, log_decay, in_state, out_state):
    length = values.shape[0]
    blocks = length // SPAN
    highest = lax.Precision.HIGHEST
    values4 = values.reshape(blocks, SPAN, H, P_SIZE)
    decay_blk = log_decay.reshape(blocks, SPAN, H).transpose(0, 2, 1)
    step_blk = step_size.reshape(blocks, SPAN, H).transpose(0, 2, 1)
    in_blk = in_state.reshape(blocks, SPAN, NST)
    out_blk = out_state.reshape(blocks, SPAN, NST)
    running = jnp.cumsum(decay_blk, axis=2)
    gap = running[:, :, :, None] - running[:, :, None, :]
    lower = jnp.tril(jnp.ones((SPAN, SPAN), dtype=bool))
    weights = jnp.where(lower, jnp.exp(jnp.where(lower, gap, 0.0)), 0.0)
    intersection = jnp.einsum("bln,bsn->bls", out_blk, in_blk, precision=highest)
    scores = weights * intersection[:, None, :, :] * step_blk[:, :, None, :]
    inner = jnp.einsum("bhls,bshp->blhp", scores, values4, precision=highest)
    to_end = jnp.exp(running[:, :, -1:] - running) * step_blk
    local = jnp.einsum("bsn,bhs,bshp->bhpn", in_blk, to_end, values4, precision=highest)
    whole_decay = jnp.exp(running[:, :, -1])

    def carry_state(state, item):
        decay_now, add_now = item
        return (state * decay_now[:, None, None] + add_now, state)

    _, prior = lax.scan(carry_state, jnp.zeros_like(local[0]), (whole_decay, local))
    outer = jnp.einsum("bln,bhpn,bhl->blhp", out_blk, prior, jnp.exp(running), precision=highest)
    return (inner + outer).reshape(length, H, P_SIZE)


def mixer(project, dt_raw, conv_weight, conv_bias, dt_bias, a_log, d_skip, gate_gain):
    length = project.shape[0]
    gate_part = project[:, :E]
    conv_in = project[:, E:]
    padded = jnp.pad(conv_in, ((CONVK - 1, 0), (0, 0)))
    conv_out = conv_bias + padded[0:length] * conv_weight[0]
    for offset in range(1, CONVK):
        conv_out = conv_out + padded[offset : offset + length] * conv_weight[offset]
    activ = jax.nn.silu(conv_out)
    values = activ[:, :E].reshape(length, H, P_SIZE)
    in_state = activ[:, E : E + NST]
    out_state = activ[:, E + NST :]
    step_size = jax.nn.softplus(dt_raw + dt_bias)
    log_decay = -jnp.exp(a_log) * step_size
    mixed = ssd_scan(values, step_size, log_decay, in_state, out_state) + d_skip[:, None] * values
    gated = mixed.reshape(length, E) * jax.nn.silu(gate_part)
    return rms_norm(gated, gate_gain)


def body(
    tokens,
    w_in,
    w_dt,
    w_out,
    norm_gain,
    conv_weight,
    conv_bias,
    dt_bias,
    a_log,
    d_skip,
    gate_gain,
    cotangent,
):
    tokens_f = tokens.astype(jnp.float32)
    normed_f, norm_pull = jax.vjp(rms_norm, tokens_f, norm_gain)
    normed = normed_f.astype(jnp.bfloat16)
    pieces = (
        lax.all_gather(w_in, "shard", axis=0, tiled=True),
        lax.all_gather(w_dt, "shard", axis=0, tiled=True),
    )
    columns = normed
    project = jnp.dot(columns, pieces[0], preferred_element_type=jnp.float32)
    dt_raw = jnp.dot(columns, pieces[1], preferred_element_type=jnp.float32)
    gated_f, mixer_pull = jax.vjp(
        mixer, project, dt_raw, conv_weight, conv_bias, dt_bias, a_log, d_skip, gate_gain
    )
    gated = gated_f.astype(jnp.bfloat16)
    columns = gated
    mixed_out = jnp.dot(
        columns,
        lax.all_gather(w_out, "shard", axis=0, tiled=True),
        preferred_element_type=jnp.float32,
    )
    result = (tokens_f + mixed_out).astype(jnp.bfloat16)
    grad_out = lax.psum_scatter(
        contract_rows(gated, cotangent).astype(jnp.bfloat16),
        "shard",
        scatter_dimension=0,
        tiled=True,
    ).astype(jnp.float32)
    back_gated = contract_cols(cotangent, lax.all_gather(w_out, "shard", axis=0, tiled=True))
    pulled = mixer_pull(back_gated)
    back_proj = pulled[0].astype(jnp.bfloat16)
    back_dt = pulled[1].astype(jnp.bfloat16)
    grad_in, grad_dt = (
        lax.psum_scatter(
            contract_rows(normed, back_proj).astype(jnp.bfloat16),
            "shard",
            scatter_dimension=0,
            tiled=True,
        ).astype(jnp.float32),
        lax.psum_scatter(
            contract_rows(normed, back_dt).astype(jnp.bfloat16),
            "shard",
            scatter_dimension=0,
            tiled=True,
        ).astype(jnp.float32),
    )
    grad_in, grad_dt, grad_out = (
        lax.psum(grad_in.astype(jnp.bfloat16), "replica").astype(jnp.float32),
        lax.psum(grad_dt.astype(jnp.bfloat16), "replica").astype(jnp.float32),
        lax.psum(grad_out.astype(jnp.bfloat16), "replica").astype(jnp.float32),
    )
    pieces = (
        lax.all_gather(w_in, "shard", axis=0, tiled=True),
        lax.all_gather(w_dt, "shard", axis=0, tiled=True),
    )
    part_cols = contract_cols(back_proj, pieces[0]) + contract_cols(back_dt, pieces[1])
    back_tokens, grad_norm = norm_pull(part_cols)
    token_grad = cotangent.astype(jnp.float32) + back_tokens
    small_grads = lax.psum(
        (grad_norm, pulled[2], pulled[3], pulled[4], pulled[5], pulled[6], pulled[7]),
        ("replica", "shard"),
    )
    return (
        result,
        token_grad,
        grad_in,
        grad_dt,
        grad_out,
        small_grads[0],
        small_grads[1],
        small_grads[2],
        small_grads[3],
        small_grads[4],
        small_grads[5],
        small_grads[6],
    )


def solution(mesh):
    placed = (
        P(("replica", "shard"), None),
        P("shard", None),
        P("shard", None),
        P("shard", None),
        P(),
        P(),
        P(),
        P(),
        P(),
        P(),
        P(),
        P(("replica", "shard"), None),
    )
    return jax.shard_map(
        body,
        mesh=mesh,
        in_specs=placed,
        out_specs=(
            P(("replica", "shard"), None),
            P(("replica", "shard"), None),
            P("shard", None),
            P("shard", None),
            P("shard", None),
            P(),
            P(),
            P(),
            P(),
            P(),
            P(),
            P(),
        ),
        check_vma=False,
    )
```

profile of v0, /device:TPU:8, one launch (start us, length us, event | category | flops | bytes accessed | tf_op | source)
XLA Modules:
  0.0 2894.5 jit_solution(18246477915600876768)
XLA Ops:
  38.6 438.9 %all-gather.3.cloned.1.call-done = bf16[2560,10496]{1,0:T(8,128)(2,1)} async-done(((bf16[640,10496]{1,0:T(8,128)(2,1)}), bf16[2560,10496]{1,0:T(8,128)(2,1)}) %all-gather.3.cloned.1.call-update) | async-done | bytes 53739536 | tf_op jit(solution)/shard_map/all_gather | solution.py:99
  477.4 65.4 %fusion.87 = f32[1024,10496]{1,0:T(8,128)} fusion(bf16[2560,10496]{1,0:T(8,128)(2,1)} %all-gather.3.cloned.1.call-done, bf16[1024,2560]{1,0:T(8,128)(2,1)} %param.16, f32[2560]{0:T(1024)S(1)} %copy-done.54, f32[1024]{0:T(1024)S(1)} %fusion.78), kind=kOutput, calls=%fused_computation.169 | convolution fusion | flops 55039754240 | bytes 101988352 | tf_op jit(solution)/shard_map/dot_general | solution.py:103
  558.9 48.1 %fusion.26 = (f32[1024,5376]{1,0:T(8,128)}, f32[1024,5376]{1,0:T(8,128)}) fusion(f32[1024,5376]{1,0:T(8,128)} %slice.71, f32[5376]{0:T(1024)S(1)} %get-tuple-element.251, f32[5376]{0:T(1024)S(1)} %get-tuple-element.252, f32[5376]{0:T(1024)S(1)} %get-tuple-element.250, f32[5376]{0:T(1024)S(1)} %get-tuple-element.249, f32[5376]{0:T(1024)S(1)} %copy-done.62), kind=kLoop, calls=%fused_computation.51 | loop fusion | flops 66060288 | bytes 66167808 | tf_op jit(solution)/shard_map/jvp(jit(silu))/mul | solution.py:70
  773.9 103.0 %fusion.33 = f32[4,256,80,64]{1,3,2,0:T(8,128)} fusion(f32[4,80,64,256]{3,2,1,0:T(8,128)S(1)} %fusion.96, f32[4,256,80]{1,2,0:T(8,128)S(1)} %copy-done.12, f32[4,80,256]{2,1,0:T(8,128)S(1)} %bitcast.216, f32[4,256,256]{2,1,0:T(8,128)S(1)} %copy-done.23, f32[4,80,256]{2,1,0:T(8,128)S(1)} %copy-done.26, pred[256,256]{1,0:T(8,128)(4,1)S(1)} %copy-done.52, ...), kind=kOutput, calls=%fused_computation.61 | convolution fusion | flops 16221470720 | bytes 65011712 | tf_op jit(solution)/shard_map/jvp(bhls,bshp->blhp)/dot_general | solution.py:48
  973.0 37.9 %multiply_reduce_fusion.8 = (f32[5120]{0:T(1024)}, f32[1024]{0:T(1024)S(1)}, f32[1024,5120]{1,0:T(8,128)}) fusion(f32[1024,5120]{1,0:T(8,128)} %get-tuple-element.294, f32[1024]{0:T(1024)S(1)} %fusion.79, f32[5120]{0:T(1024)S(1)} %copy-done.63, bf16[1024,2560]{1,0:T(8,128)(2,1)} %param.27, bf16[5120,2560]{1,0:T(8,128)(2,1)} %all-gather.5.cloned.1.call-done), kind=kOutput, calls=%fused_computation.68 | convolution fusion | flops 26874998784 | bytes 73449472 | tf_op jit(solution)/shard_map/dot_general | solution.py:28
  1010.9 50.2 %multiply_reduce_fusion.9 = (f32[5120]{0:T(1024)}, f32[1024,5120]{1,0:T(8,128)}, f32[1024,5120]{1,0:T(8,128)}) fusion(f32[1024,5376]{1,0:T(8,128)} %get-tuple-element.295, f32[1024,10496]{1,0:T(8,128)} %fusion.87, f32[1024,5120]{1,0:T(8,128)} %get-tuple-element.294, f32[1024]{0:T(1024)S(1)} %multiply_multiply_fusion.2, f32[1024]{0:T(1024)S(1)} %fusion.79, ...), kind=kLoop, calls=%fused_computation.69 | loop fusion | flops 110095360 | bytes 146870272 | tf_op jit(solution)/shard_map/transpose(jvp())/reduce_sum | solution.py:76
  1135.7 136.2 %fusion.11 = (f32[4,80,256]{2,1,0:T(8,128)}, f32[4,80,256]{2,1,0:T(8,128)}, f32[4,80,256]{2,1,0:T(8,128)}, f32[4,256,256]{2,1,0:T(8,128)}) fusion(f32[4,80,256]{2,1,0:T(8,128)S(1)} %bitcast.217, f32[4,256,256]{2,1,0:T(8,128)S(1)} %copy-done.24, f32[4,80,256]{2,1,0:T(8,128)S(1)} %copy-done.27, pred[256,256]{1,0:T(8,128)(4,1)S(1)} %copy-done.53, ...), kind=kOutput, calls=%fused_computation.23 | convolution fusion | flops 16420192256 | bytes 45744128 | tf_op jit(solution)/shard_map/transpose(jvp(bhls,bshp->blhp))/dot_general | solution.py:48
  1271.9 76.8 %fusion.6 = f32[4,80,64,256]{3,2,1,0:T(8,128)} fusion(f32[4,80,256]{2,1,0:T(8,128)S(1)} %bitcast.218, f32[4,256,256]{2,1,0:T(8,128)S(1)} %copy-done.24, f32[4,80,256]{2,1,0:T(8,128)S(1)} %copy-done.27, pred[256,256]{1,0:T(8,128)(4,1)S(1)} %copy-done.53, f32[4,80,64,256]{3,0,2,1:T(4,128)S(1)} %bitcast.191), kind=kOutput, calls=%fused_computation.19 | convolution fusion | flops 16210984960 | bytes 43712512 | tf_op jit(solution)/shard_map/transpose(jvp(bhls,bshp->blhp))/dot_general | solution.py:48
  1385.2 36.5 %while.35 = (s32[]{:T(128)}, f32[80,64,128]{2,1,0:T(8,128)}, f32[4,80]{1,0:T(4,128)S(1)}, f32[4,80,64,128]{3,1,2,0:T(8,128)}, f32[4,80,64,128]{3,2,1,0:T(8,128)}...) while((s32[]{:T(128)}, f32[80,64,128]{2,1,0:T(8,128)}, ...), condition=%wide.region_10.11_spmd.clone, body=%wide.region_8.10_spmd.clone.sunk | while | flops 3276724 | bytes 18352148 | solution.py:57
  1421.9 34.9 %bitcast_add_fusion.2 = (f32[4,256,80,64]{1,2,3,0:T(8,128)}, f32[4,256,80,64]{1,2,3,0:T(8,128)}) fusion(f32[4,80,64,256]{3,2,1,0:T(8,128)} %fusion.6, f32[4,256,80]{1,2,0:T(8,128)S(1)} %copy-done.19, f32[4,256,128,1]{2,1,3,0:T(8,128)S(1)} %bitcast.204, f32[4,80,64,128]{3,1,2,0:T(8,128)} %get-tuple-element.189), kind=kOutput, calls=%fused_computation.55 | convolution fusion | flops 8063549440 | bytes 74252288 | tf_op jit(solution)/shard_map/transpose(jvp(bsn,bhs,bshp->bhpn))/dot_general | solution.py:50
  1500.6 35.7 %convolution_convert_fusion.1 = bf16[5120,2560]{1,0:T(8,128)(2,1)} fusion(bf16[1024,2560]{1,0:T(8,128)(2,1)} %param.27, f32[1024,5120]{1,0:T(8,128)} %get-tuple-element.294, f32[5120]{0:T(1024)S(1)} %copy-done.64, f32[1024]{0:T(1024)S(1)} %copy-done.68), kind=kOutput, calls=%fused_computation.40 | convolution fusion | flops 26872381440 | bytes 52453376 | tf_op jit(solution)/shard_map/dot_general | solution.py:22
  1536.3 36.8 %copy.190 = f32[4,256,80,64]{3,2,1,0:T(8,128)} copy(f32[4,256,80,64]{1,2,3,0:T(8,128)} %get-tuple-element.316) | data formatting | bytes 41943040 | tf_op jit(solution)/shard_map/transpose(jvp())/reshape | solution.py:37
  1606.3 40.5 %fusion.59 = f32[4,256,128]{2,1,0:T(8,128)S(1)} fusion(f32[4,80,64,128]{3,2,1,0:T(8,128)} %get-tuple-element.486, f32[4,256,80,64]{1,0,3,2:T(4,128)} %reshape.225, f32[4,256,80]{1,2,0:T(8,128)S(1)} %copy-done.14), kind=kOutput, calls=%fused_computation.111 | convolution fusion | flops 8058306560 | bytes 32309248 | tf_op jit(solution)/shard_map/transpose(jvp(bln,bhpn,bhl->blhp))/dot_general | solution.py:58
  1647.9 37.0 %convolution_bitcast_fusion = f32[4,256,128]{2,1,0:T(8,128)S(1)} fusion(f32[4,256,80,64]{1,2,3,0:T(8,128)} %copy-done.2, f32[4,80,64,128]{3,1,2,0:T(8,128)} %get-tuple-element.189), kind=kOutput, calls=%fused_computation.112 | convolution fusion | flops 8053063680 | bytes 31981568 | tf_op jit(solution)/shard_map/transpose(jvp(bsn,bhs,bshp->bhpn))/dot_general | solution.py:50
  1704.6 56.3 %multiply_reduce_fusion.4 = (f32[5376]{0:T(1024)S(1)}, f32[5376]{0:T(1024)S(1)}, f32[5376]{0:T(1024)S(1)}, f32[5376]{0:T(1024)}, f32[5376]{0:T(1024)S(1)}, /*index=5*/f32[1024,5376]{1,0:T(8,128)}) fusion(f32[1024,5376]{1,0:T(8,128)} %slice.71, f32[1024,10496]{1,0:T(8,128)} %fusion.87, f32[1024,5376]{1,0:T(8,128)} %get-tuple-element.296, ...), kind=kLoop, calls=%fused_computation.48 | loop fusion | flops 110073600 | bytes 110208000 | tf_op jit(solution)/shard_map/transpose(jvp())/reduce_sum | solution.py:69
  1760.9 34.7 %broadcast_multiply_fusion = (f32[1024,5376]{1,0:T(8,128)}, f32[1024,5376]{1,0:T(8,128)}, f32[1024,5376]{1,0:T(8,128)}, f32[1024,5376]{1,0:T(8,128)}) fusion(f32[1024,5376]{1,0:T(8,128)} %get-tuple-element.292, f32[5376]{0:T(1024)S(1)} %copy-done.41, f32[5376]{0:T(1024)S(1)} %copy-done.37, f32[5376]{0:T(1024)S(1)} %copy-done.39, f32[5376]{0:T(1024)S(1)} %copy-done.43), kind=kLoop, calls=%fused_computation.92 | loop fusion | flops 22020096 | bytes 110186496 | tf_op jit(solution)/shard_map/transpose(jvp())/mul | solution.py:69
  1795.6 36.1 %pad_add_fusion = f32[1024,5376]{1,0:T(8,128)} fusion(f32[1024,5376]{1,0:T(8,128)} %get-tuple-element.302, f32[1024,5376]{1,0:T(8,128)} %get-tuple-element.303, f32[1024,5376]{1,0:T(8,128)} %get-tuple-element.304, f32[1024,5376]{1,0:T(8,128)} %get-tuple-element.301), kind=kLoop, calls=%fused_computation.43 | loop fusion | flops 16515072 | bytes 110100480 | tf_op jit(solution)/shard_map/transpose(jvp())/add_any | solution.py:67
  1831.7 71.7 %convolution_convert_fusion = bf16[2560,10496]{1,0:T(8,128)(2,1)} fusion(f32[1024,5120]{1,0:T(8,128)} %get-tuple-element.300, f32[1024,5376]{1,0:T(8,128)} %pad_add_fusion, bf16[1024,2560]{1,0:T(8,128)(2,1)} %param.16, f32[2560]{0:T(1024)S(1)} %copy-done.56, f32[1024]{0:T(1024)S(1)} %copy-done.61), kind=kOutput, calls=%fused_computation.21 | convolution fusion | flops 55088119808 | bytes 101988352 | tf_op jit(solution)/shard_map/dot_general | solution.py:22
  1905.2 450.1 %reduce-scatter.6.cloned.1.call-done = bf16[640,10496]{1,0:T(8,128)(2,1)} async-done(((bf16[2560,10496]{1,0:T(8,128)(2,1)}), bf16[640,10496]{1,0:T(8,128)(2,1)}) %reduce-scatter.6.cloned.1.call-update) | async-done | bytes 13434896 | tf_op jit(solution)/shard_map/reduce_scatter | solution.py:127
  2355.5 72.5 %fusion.58 = f32[1024,2560]{1,0:T(8,128)} fusion(bf16[2560,10496]{1,0:T(8,128)(2,1)} %all-gather.3.cloned.1.call-done, f32[1024,5120]{1,0:T(8,128)} %get-tuple-element.300, f32[1024,5376]{1,0:T(8,128)} %pad_add_fusion), kind=kOutput, calls=%fused_computation.108 | convolution fusion | flops 55050764288 | bytes 107216896 | tf_op jit(solution)/shard_map/dot_general | solution.py:28
  2452.0 38.7 %fusion.48 = bf16[1024,2560]{1,0:T(8,128)(2,1)} fusion(bf16[1024,2560]{1,0:T(8,128)(2,1)S(1)} %bitcast.197, bf16[5120,2560]{1,0:T(8,128)(2,1)} %all-gather.5.cloned.1.call-done, f32[1024,5120]{1,0:T(8,128)} %get-tuple-element.294, f32[5120]{0:T(1024)S(1)} %copy-done.65, f32[1024]{0:T(1024)S(1)} %copy-done.69), kind=kOutput, calls=%fused_computation.100 | convolution fusion | flops 26867138560 | bytes 57696256 | tf_op jit(solution)/shard_map/dot_general | solution.py:110
  2490.9 42.4 %all-reduce.16 = (f32[2560]{0:T(1024)}, f32[5376]{0:T(1024)}, f32[80]{0:T(128)}, f32[80]{0:T(128)}, f32[80]{0:T(128)}, /*index=5*/f32[5120]{0:T(1024)}) all-reduce(f32[2560]{0:T(1024)S(1)} %get-tuple-element.247, f32[5376]{0:T(1024)S(1)} %copy-done.47, ...), channel_id=1, replica_groups=mesh['replica'=8,'shard'=4] {'replica','shard'}, use_global_device_ids=true, to_apply=%region_25.26 | all-reduce | flops 13296 | bytes 106368 | tf_op jit(solution)/shard_map/psum | solution.py:152
  2533.3 224.0 %all-reduce.23.cloned.1.call-done = (bf16[640,10496]{1,0:T(8,128)(2,1)}, bf16[640,80]{0,1:T(8,128)(2,1)}, bf16[1280,2560]{1,0:T(8,128)(2,1)}) async-done(((bf16[640,10496]{1,0:T(8,128)(2,1)}, bf16[640,80]{0,1:T(8,128)(2,1)}, bf16[1280,2560]{1,0:T(8,128)(2,1)}), (bf16[640,10496]{1,0:T(8,128)(2,1)}, bf16[640,80]{0,1:T(8,128)(2,1)}, bf16[1280,2560]{1,0:T(8,128)(2,1)})) %all-reduce.23.cloned.1.call-update) | async-done | bytes 20090896 | tf_op jit(solution)/shard_map/psum | solution.py:141
  2778.5 107.4 %all-reduce.21.cloned.1.call-done = f32[4,5376]{1,0:T(4,128)} async-done(((f32[4,5376]{1,0:T(4,128)}), f32[4,5376]{1,0:T(4,128)}) %all-reduce.21.cloned.1.call-update) | async-done | bytes 86032 | tf_op jit(solution)/shard_map/psum | solution.py:152
  (305 shorter events, 621.5 us)
Async XLA Ops:
  7.2 470.2 %all-gather.3.cloned.1.call-start = ((), (), s32[]{:S(2)}) async-start(), calls=%async_computation.3 | async-start | bytes 67174400 | tf_op jit(solution)/shard_map/all_gather | solution.py:99
  8.0 965.0 %all-gather.5.cloned.1.call-start = ((), (), s32[]{:S(2)}) async-start(), calls=%async_computation.4 | async-start | bytes 32768000 | tf_op jit(solution)/shard_map/all_gather | solution.py:112
  8.7 1894.8 %reduce-scatter.10.cloned.1.call-start = ((), (), s32[]{:S(2)}) async-start(), calls=%async_computation.8 | async-start | bytes 819200
  13.0 529.8 %copy-start.59 = (f32[1024]{0:T(1024)}, f32[1024]{0:T(1024)S(1)}, u32[]{:S(2)}) copy-start(f32[1024]{0:T(1024)S(1)} %fusion.78) | copy-start | bytes 12292
  13.3 545.6 %copy-start.36 = (f32[5376]{0:T(1024)}, f32[5376]{0:T(1024)S(1)}, u32[]{:S(2)}) copy-start(f32[5376]{0:T(1024)S(1)} %get-tuple-element.249) | copy-start | bytes 64516
  13.3 545.6 %copy-start.38 = (f32[5376]{0:T(1024)}, f32[5376]{0:T(1024)S(1)}, u32[]{:S(2)}) copy-start(f32[5376]{0:T(1024)S(1)} %get-tuple-element.250) | copy-start | bytes 64516
  13.3 545.6 %copy-start.40 = (f32[5376]{0:T(1024)}, f32[5376]{0:T(1024)S(1)}, u32[]{:S(2)}) copy-start(f32[5376]{0:T(1024)S(1)} %get-tuple-element.251) | copy-start | bytes 64516
  13.3 545.6 %copy-start.42 = (f32[5376]{0:T(1024)}, f32[5376]{0:T(1024)S(1)}, u32[]{:S(2)}) copy-start(f32[5376]{0:T(1024)S(1)} %get-tuple-element.252) | copy-start | bytes 64516
  30.6 512.3 %copy-start.15 = (f32[1024,80]{0,1:T(8,128)}, f32[1024,80]{0,1:T(8,128)S(1)}, u32[]{:S(2)}) copy-start(f32[1024,80]{0,1:T(8,128)S(1)} %get-tuple-element.312) | copy-start | bytes 983044
  33.3 509.6 %copy-start.10 = (f32[4,80,2,128]{3,1,2,0:T(8,128)}, f32[4,80,2,128]{3,1,2,0:T(8,128)S(1)}, u32[]{:S(2)}) copy-start(f32[4,80,2,128]{3,1,2,0:T(8,128)S(1)} %reduce-window.14) | copy-start | bytes 983044
  33.6 509.3 %copy-start.44 = (f32[4,80,2]{1,2,0:T(2,128)}, f32[4,80,2]{1,2,0:T(2,128)S(1)}, u32[]{:S(2)}) copy-start(f32[4,80,2]{1,2,0:T(2,128)S(1)} %copy.144) | copy-start | bytes 7684
  34.8 508.1 %copy-start.50 = (f32[4,80]{1,0:T(4,128)}, f32[4,80]{1,0:T(4,128)S(1)}, u32[]{:S(2)}) copy-start(f32[4,80]{1,0:T(4,128)S(1)} %slice_reduce_fusion) | copy-start | bytes 3844
  671.6 74.1 %copy-start.5 = (f32[1024,128]{1,0:T(8,128)}, f32[1024,128]{1,0:T(8,128)S(1)}, u32[]{:S(2)}) copy-start(f32[1024,128]{1,0:T(8,128)S(1)} %get-tuple-element.305) | copy-start | bytes 1572868
  1500.5 404.7 %reduce-scatter.8.cloned.1.call-start = ((), (), s32[]{:S(2)}) async-start(), calls=%async_computation.6 | async-start | bytes 32768000 | tf_op jit(solution)/shard_map/reduce_scatter | solution.py:116
  1536.3 819.1 %reduce-scatter.6.cloned.1.call-start = ((), (), s32[]{:S(2)}) async-start(), calls=%async_computation.5 | async-start | bytes 67174400 | tf_op jit(solution)/shard_map/reduce_scatter | solution.py:127
  1606.3 80.5 %slice-start = ((s8[20971520]{0:T(1024)(128)(4,1)}), s8[4194304]{0:T(1024)(128)(4,1)S(1)}, s32[]{:S(2)}) async-start(s8[20971520]{0:T(1024)(128)(4,1)} %bitcast.192), calls=%async_computation.10 | async-start | bytes 8388608
  1606.3 80.5 %slice-start.1 = ((s8[20971520]{0:T(1024)(128)(4,1)}), s8[4194304]{0:T(1024)(128)(4,1)S(1)}, s32[]{:S(2)}) async-start(s8[20971520]{0:T(1024)(128)(4,1)} %bitcast.192), calls=%async_computation.11 | async-start | bytes 8388608
  1606.3 80.5 %slice-start.2 = ((s8[20971520]{0:T(1024)(128)(4,1)}), s8[4194304]{0:T(1024)(128)(4,1)S(1)}, s32[]{:S(2)}) async-start(s8[20971520]{0:T(1024)(128)(4,1)} %bitcast.192), calls=%async_computation.12 | async-start | bytes 8388608
  1606.3 80.5 %slice-start.3 = ((s8[20971520]{0:T(1024)(128)(4,1)}), s8[4194304]{0:T(1024)(128)(4,1)S(1)}, s32[]{:S(2)}) async-start(s8[20971520]{0:T(1024)(128)(4,1)} %bitcast.192), calls=%async_computation.13 | async-start | bytes 8388608
  1704.6 56.3 %copy-start.43 = (f32[5376]{0:T(1024)S(1)}, f32[5376]{0:T(1024)}, u32[]{:S(2)}) copy-start(f32[5376]{0:T(1024)} %copy-done.42) | copy-start | bytes 64516
  1903.4 853.9 %all-reduce.23.cloned.1.call-start = ((), (), s32[]{:S(2)}) async-start(), calls=%async_computation.9 | async-start | bytes 40181760 | tf_op jit(solution)/shard_map/psum | solution.py:141
  2355.4 72.6 %copy-start.21 = (bf16[2560,80]{0,1:T(8,128)(2,1)S(1)}, bf16[2560,80]{0,1:T(8,128)(2,1)}, u32[]{:S(2)}) copy-start(bf16[2560,80]{0,1:T(8,128)(2,1)} %copy-done.20) | copy-start | bytes 1228804
  2355.4 72.6 %copy-start.29 = (bf16[1024,80]{0,1:T(8,128)(2,1)S(1)}, bf16[1024,80]{0,1:T(8,128)(2,1)}, u32[]{:S(2)}) copy-start(bf16[1024,80]{0,1:T(8,128)(2,1)} %copy-done.28) | copy-start | bytes 491524
  2355.4 530.5 %all-reduce.21.cloned.1.call-start = ((), (), s32[]{:S(2)}) async-start(), calls=%async_computation.7 | async-start | bytes 172032 | tf_op jit(solution)/shard_map/psum | solution.py:152
  (68 other events, 1916.6 us)
Sparse Core Ops, SparseCore 0:
  9.9 467.4 all-gather.2
  479.3 236.3 all-gather.4
  1500.7 25.7 reduce-scatter.9
  1536.4 230.6 reduce-scatter.7
  1903.5 451.8 reduce-scatter.5
  2358.9 398.3 all-reduce.22
  2763.5 122.3 all-reduce.20
where the time goes:
time: 2900 us; the launch traced here: 2890 us
  waiting for transfers between devices  1220 us (42%)
  matrix products  853 us (29%)
  other arithmetic  441 us (15%)
  local copies, waits for them, and re-layouts  311 us (11%)
  blocking collectives  52.3 us (2%)
    reduce_scatter x1, waiting for transfers between devices, body(): lax.psum_scatter(contract_rows(normed, back_proj).astype(jnp.bfloat16), '...  450 us
    all_gather x1, waiting for transfers between devices, body(): lax.all_gather(w_in, 'shard', axis=0, tiled=True)  439 us
    dot_general x3, matrix products, ssd_scan(): inner = jnp.einsum('bhls,bshp->blhp', scores, values4, precision=highest)  316 us
    psum x1, waiting for transfers between devices, body(): lax.psum(grad_in.astype(jnp.bfloat16), 'replica').astype(jnp.float32)  224 us
    dot_general x3, matrix products, contract_cols(): lax.dot_general(left, right, (((1,), (1,)), ((), ())), preferred_element_...  120 us
    dot_general x3, matrix products, contract_rows(): lax.dot_general(left, right, (((0,), (0,)), ((), ())), preferred_element_...  111 us
    psum x1, waiting for transfers between devices, body(): lax.psum((grad_norm, pulled[2], pulled[3], pulled[4], pulled[5], pulled[6...  107 us
    dot_general x3, matrix products, ssd_scan(): jnp.einsum('bsn,bhs,bshp->bhpn', in_blk, to_end, values4, precision=highest)  99.6 us
  transfers between devices with their start and end apart: 7, of which 4 were waited for; matrix products, arithmetic and copies ran while one was open for 37% of the time, Pallas kernels for 0%

commit v1 on v0

v1 whole, which is shorter than its diff:
```python
import functools
import jax
import jax.numpy as jnp
import numpy as np
from jax import lax
from jax.experimental import pallas as pl
from jax.experimental.pallas import tpu as pltpu
from jax.sharding import Mesh
from jax.sharding import PartitionSpec as P

H = 80
P_SIZE = 64
E = 5120
NST = 128
CONVK = 4
EPS = 1e-05
Q = 128
CB = 512
HB = CB // P_SIZE
LOG2E = 1.4426950408889634
F32 = jnp.float32
BF16 = jnp.bfloat16
NT = (((1,), (1,)), ((), ()))
TN = (((0,), (0,)), ((), ()))
NN = (((1,), (0,)), ((), ()))


def mm(a, b, dims=NN):
    return lax.dot_general(a, b, dims, preferred_element_type=F32)


def mm_exact(a, b, dims=NN):
    return lax.dot_general(a, b, dims, precision=lax.Precision.HIGHEST, preferred_element_type=F32)


def shifted(before, now):
    stacked = jnp.concatenate([before, now], axis=0)
    return [pltpu.roll(stacked, k, 0)[8:] for k in (1, 2, 3)]


def rows_before(ref, start, lanes):
    prev = ref[pl.ds(pl.multiple_of(jnp.maximum(start - 8, 0), 8), 8), lanes]
    return jnp.where(start > 0, prev, 0.0)


def conv_of(now, past, taps, bias):
    return (
        bias
        + past[2] * taps[0:1]
        + past[1] * taps[1:2]
        + past[0] * taps[2:3]
        + now * taps[3:4]
    )


def fold8(x):
    total = x[0:8]
    for k in range(1, x.shape[0] // 8):
        total = total + x[8 * k : 8 * k + 8]
    return total


def lower_tri():
    return lax.broadcasted_iota(jnp.int32, (Q, Q), 0) >= lax.broadcasted_iota(jnp.int32, (Q, Q), 1)


def prepare_kernel(ps_ref, cw_ref, cb_ref, dtb_ref, al_ref, b_ref, c_ref, bt_ref, ct_ref, g_ref, run_ref, step_ref):
    tri = lower_tri()
    ones = tri.astype(F32)

    def chunk(c, carry):
        start = pl.multiple_of(c * Q, Q)
        rows = pl.ds(start, Q)
        state = []
        for j in range(2):
            lanes = slice(NST * j, NST * (j + 1))
            now = ps_ref[rows, lanes]
            past = shifted(rows_before(ps_ref, start, lanes), now)
            co = conv_of(now, past, cw_ref[:, lanes], cb_ref[:, lanes])
            state.append(co * jax.nn.sigmoid(co))
        ins, outs = state
        b_ref[rows, :] = ins.astype(BF16)
        c_ref[rows, :] = outs.astype(BF16)
        bt_ref[:, rows] = ins.T.astype(BF16)
        ct_ref[:, rows] = outs.T.astype(BF16)
        g_ref[rows, :] = jnp.where(tri, mm_exact(outs, ins, NT), 0.0)
        step = jax.nn.softplus(ps_ref[rows, 2 * NST : 3 * NST] + dtb_ref[...])
        decay = -jnp.exp(al_ref[...]) * step
        run = mm_exact(ones, decay) * LOG2E
        run_ref[:, rows] = run.T
        step_ref[:, rows] = step.T
        return carry

    lax.fori_loop(0, ps_ref.shape[0] // Q, chunk, 0)


def prepare(ps, cw, cb, dtb, al):
    tokens = ps.shape[0]
    return pl.pallas_call(
        prepare_kernel,
        out_shape=(
            jax.ShapeDtypeStruct((tokens, NST), BF16),
            jax.ShapeDtypeStruct((tokens, NST), BF16),
            jax.ShapeDtypeStruct((NST, tokens), BF16),
            jax.ShapeDtypeStruct((NST, tokens), BF16),
            jax.ShapeDtypeStruct((tokens, Q), F32),
            jax.ShapeDtypeStruct((128, tokens), F32),
            jax.ShapeDtypeStruct((128, tokens), F32),
        ),
        compiler_params=pltpu.CompilerParams(vmem_limit_bytes=40 << 20),
        cost_estimate=pl.CostEstimate(flops=600000000, bytes_accessed=int(5e6), transcendentals=1000000),
        name="prepare",
    )(ps, cw, cb, dtb, al)


def pair_select(first, cols, j):
    return jnp.where(first, cols[:, 2 * j : 2 * j + 1], cols[:, 2 * j + 1 : 2 * j + 2])


def forward_kernel(
    both_ref, bg_ref, run_ref, step_ref, c_ref, bt_ref, g_ref, cw_ref, cb_ref, dsk_ref, gain_ref,
    mixed_ref, y_ref, prior_ref, ss_ref, cg_ref, state,
):
    first = lax.broadcasted_iota(jnp.int32, (1, 128), 1) < P_SIZE
    state[...] = jnp.zeros_like(state)

    @pl.when(pl.program_id(0) == 0)
    def _():
        ss_ref[...] = jnp.zeros_like(ss_ref)
        cg_ref[...] = jnp.zeros_like(cg_ref)

    def chunk(c, carry):
        start = pl.multiple_of(c * Q, Q)
        rows = pl.ds(start, Q)
        run_rows = run_ref[:, rows]
        run_cols = run_rows.T
        step_cols = step_ref[:, rows].T
        run_end = run_cols[Q - 1 : Q, :]
        outs = c_ref[rows, :]
        ins_t = bt_ref[:, rows]
        meet = g_ref[rows, :]
        squares = jnp.zeros((Q, 128), F32)
        products = jnp.zeros((Q, 128), F32)
        for j in range(CB // 128):
            lanes = slice(128 * j, 128 * (j + 1))
            below = slice(CB + 128 * j, CB + 128 * (j + 1))
            now = both_ref[rows, below].astype(F32)
            past = shifted(rows_before(both_ref, start, below).astype(F32), now)
            co = conv_of(now, past, cw_ref[:, lanes], cb_ref[:, lanes])
            values = co * jax.nn.sigmoid(co)
            run_pair = pair_select(first, run_cols, j)
            end_pair = pair_select(first, run_end, j)
            weighted = pair_select(first, step_cols, j) * values
            stacked = jnp.concatenate(
                [jnp.where(first, weighted, 0.0), jnp.where(first, 0.0, weighted)], axis=0
            ).astype(BF16)
            scores = []
            for h in (2 * j, 2 * j + 1):
                gap = run_cols[:, h : h + 1] - run_rows[h : h + 1, :]
                scores.append((jnp.exp2(jnp.minimum(gap, 0.0)) * meet).astype(BF16))
            inner = mm(jnp.concatenate(scores, axis=1), stacked)
            held = state[:, lanes]
            held_b = held.astype(BF16)
            outer = mm(outs, held_b) * jnp.exp2(run_pair)
            mixed = inner + outer + dsk_ref[:, lanes] * values
            gate = both_ref[rows, lanes].astype(F32)
            y = mixed * (gate * jax.nn.sigmoid(gate))
            mixed_ref[rows, lanes] = mixed.astype(BF16)
            y_ref[rows, lanes] = y.astype(BF16)
            squares = squares + y * y
            products = products + bg_ref[rows, lanes].astype(F32) * gain_ref[:, lanes] * y
            prior_ref[rows, lanes] = held_b
            add = mm(ins_t, (jnp.exp2(end_pair - run_pair) * weighted).astype(BF16))
            state[:, lanes] = held * jnp.exp2(end_pair) + add
        ss_ref[rows, :] += squares
        cg_ref[rows, :] += products
        return carry

    lax.fori_loop(0, both_ref.shape[0] // Q, chunk, 0)


def forward(proj, bg, col0, prep, cw, cb, dsk, gain):
    tokens, width = proj.shape[0], proj.shape[1] // 2
    steps = width // CB
    first = col0 // CB
    ins, outs, ins_t, outs_t, meet, run, step = prep

    def whole(shape):
        return pl.BlockSpec(shape, lambda i: (0, 0))

    def cols(rows, base, wide=CB):
        return pl.BlockSpec((rows, wide), lambda i: (0, i + base))

    def heads():
        return pl.BlockSpec((HB, tokens), lambda i: (i + first, 0))

    return pl.pallas_call(
        forward_kernel,
        grid=(steps,),
        in_specs=[
            cols(tokens, 0, 2 * CB), cols(tokens, first), heads(), heads(),
            whole((tokens, NST)), whole((NST, tokens)), whole((tokens, Q)),
            cols(CONVK, first), cols(1, first), cols(1, first), cols(1, first),
        ],
        out_specs=[
            cols(tokens, 0), cols(tokens, 0), cols(tokens, 0), whole((tokens, 128)), whole((tokens, 128)),
        ],
        out_shape=(
            jax.ShapeDtypeStruct((tokens, width), BF16),
            jax.ShapeDtypeStruct((tokens, width), BF16),
            jax.ShapeDtypeStruct((tokens, width), BF16),
            jax.ShapeDtypeStruct((tokens, 128), F32),
            jax.ShapeDtypeStruct((tokens, 128), F32),
        ),
        scratch_shapes=[pltpu.VMEM((NST, CB), F32)],
        compiler_params=pltpu.CompilerParams(vmem_limit_bytes=48 << 20),
        cost_estimate=pl.CostEstimate(
            flops=int(tokens * width * 4000), bytes_accessed=int(tokens * width * 18), transcendentals=int(tokens * width * 5)
        ),
        name="forward",
    )(proj, bg, run, step, outs, ins_t, meet, cw, cb, dsk, gain)


def backward_kernel(
    head0,
    both_ref, bg_ref, mixed_ref, prior_ref, run_ref, step_ref, b_ref, c_ref, ct_ref, g_ref, r_ref, k_ref,
    cw_ref, cb_ref, dsk_ref, gain_ref,
    dboth_ref, f_ref, ds_ref, dg_ref, dc_ref, db_ref, vec_ref, dstate, ahead,
):
    first = lax.broadcasted_iota(jnp.int32, (1, 128), 1) < P_SIZE
    last_row = lax.broadcasted_iota(jnp.int32, (Q, 1), 0) == Q - 1
    dstate[...] = jnp.zeros_like(dstate)
    ahead[...] = jnp.zeros_like(ahead)
    vec_ref[...] = jnp.zeros_like(vec_ref)

    @pl.when(pl.program_id(0) == 0)
    def _():
        for ref in (f_ref, ds_ref, dg_ref, dc_ref, db_ref):
            ref[...] = jnp.zeros_like(ref)

    head = lax.broadcasted_iota(jnp.int32, (CB, 128), 0) // P_SIZE + (head0 + HB * pl.program_id(0))
    pick = (head == lax.broadcasted_iota(jnp.int32, (CB, 128), 1)).astype(BF16)
    count = both_ref.shape[0] // Q

    def chunk(i, carry):
        c = count - 1 - i
        start = pl.multiple_of(c * Q, Q)
        rows = pl.ds(start, Q)
        run_rows = run_ref[:, rows]
        run_cols = run_rows.T
        step_cols = step_ref[:, rows].T
        run_end = run_cols[Q - 1 : Q, :]
        outs = c_ref[rows, :]
        ins = b_ref[rows, :]
        outs_t = ct_ref[:, rows]
        meet = g_ref[rows, :]
        scale = r_ref[rows, :]
        pull = k_ref[rows, :]
        dmeet = jnp.zeros((Q, Q), F32)
        douts = jnp.zeros((Q, NST), F32)
        dins = jnp.zeros((Q, NST), F32)
        runs_hi, runs_lo, steps_hi, steps_lo = [], [], [], []
        for j in range(CB // 128):
            lanes = slice(128 * j, 128 * (j + 1))
            below = slice(CB + 128 * j, CB + 128 * (j + 1))
            now = both_ref[rows, below].astype(F32)
            past = shifted(rows_before(both_ref, start, below).astype(F32), now)
            taps = cw_ref[:, lanes]
            co = conv_of(now, past, taps, cb_ref[:, lanes])
            co_sig = jax.nn.sigmoid(co)
            values = co * co_sig
            gate = both_ref[rows, lanes].astype(F32)
            gate_sig = jax.nn.sigmoid(gate)
            gate_silu = gate * gate_sig
            mixed = mixed_ref[rows, lanes].astype(F32)
            y = mixed * gate_silu
            scaled = bg_ref[rows, lanes].astype(F32) * scale
            vec_ref[40:48, lanes] += fold8(scaled * y)
            dy = scaled * gain_ref[:, lanes] - y * pull
            dmix = dy * gate_silu
            dgate = dy * mixed * (gate_sig + gate_silu * (1.0 - gate_sig))
            dboth_ref[rows, lanes] = dgate.astype(BF16)
            vec_ref[48:56, lanes] += fold8(dmix * values)

            run_pair = pair_select(first, run_cols, j)
            end_pair = pair_select(first, run_end, j)
            step_pair = pair_select(first, step_cols, j)
            weighted = step_pair * values
            stacked = jnp.concatenate(
                [jnp.where(first, weighted, 0.0), jnp.where(first, 0.0, weighted)], axis=0
            ).astype(BF16)
            rounded = weighted.astype(BF16).astype(F32)
            dmix_b = dmix.astype(BF16)
            fade_in = jnp.exp2(run_pair)
            fade_out = jnp.exp2(end_pair - run_pair)
            dmix_in = (fade_in * dmix).astype(BF16)
            kept = (fade_out * weighted).astype(BF16)
            prior = prior_ref[rows, lanes]
            dnext = dstate[:, lanes]
            dnext_b = dnext.astype(BF16)
            outer = mm(outs, prior)
            dkept = mm(ins, dnext_b)
            fades, scores = [], []
            for h in (2 * j, 2 * j + 1):
                gap = run_cols[:, h : h + 1] - run_rows[h : h + 1, :]
                fade = jnp.exp2(jnp.minimum(gap, 0.0))
                fades.append(fade)
                scores.append((fade * meet).astype(BF16))
            scores = jnp.concatenate(scores, axis=1)
            inner = mm(scores, stacked)
            both = mm(scores, dmix_b, TN)
            dinner = jnp.where(first, both[:Q], both[Q:])
            dscores = mm(dmix_b, stacked, NT)
            dmeet = dmeet + dscores[:, :Q] * fades[0] + dscores[:, Q:] * fades[1]
            kept_flow = kept.astype(F32) * dkept
            end_decay = jnp.exp2(end_pair)
            at_end = jnp.sum(kept_flow, axis=0, keepdims=True) + end_decay * jnp.sum(
                dnext * prior.astype(F32), axis=0, keepdims=True
            )
            flow = (
                dmix_b.astype(F32) * inner
                + dmix_in.astype(F32) * outer
                - rounded * dinner
                - kept_flow
                + jnp.where(last_row, at_end, 0.0)
            )
            flow_hi = flow.astype(BF16)
            runs_hi.append(flow_hi)
            runs_lo.append((flow - flow_hi.astype(F32)).astype(BF16))
            dweighted = dinner + fade_out * dkept
            dstep = dweighted * values
            dstep_hi = dstep.astype(BF16)
            steps_hi.append(dstep_hi)
            steps_lo.append((dstep - dstep_hi.astype(F32)).astype(BF16))
            dvalues = step_pair * dweighted + dsk_ref[:, lanes] * dmix
            dco = dvalues * (co_sig + values * (1.0 - co_sig))
            for k, source in enumerate((past[2], past[1], past[0], now)):
                vec_ref[8 * k : 8 * k + 8, lanes] += fold8(dco * source)
            vec_ref[32:40, lanes] += fold8(dco)
            spread = jnp.concatenate([dco, ahead[:, lanes]], axis=0)
            ahead[:, lanes] = dco[0:8]
            dconv = dco * taps[3:4]
            for k in (1, 2, 3):
                dconv = dconv + pltpu.roll(spread, Q + 8 - k, 0)[:Q] * taps[3 - k : 4 - k]
            dboth_ref[rows, below] = dconv.astype(BF16)
            douts = douts + mm(dmix_in, prior, NT)
            dins = dins + mm(kept, dnext_b, NT)
            dstate[:, lanes] = dnext * end_decay + mm(outs_t, dmix_in)
        dg_ref[rows, :] += dmeet
        dc_ref[rows, :] += douts
        db_ref[rows, :] += dins
        f_ref[rows, :] += mm(jnp.concatenate(runs_hi, axis=1), pick) + mm(jnp.concatenate(runs_lo, axis=1), pick)
        ds_ref[rows, :] += mm(jnp.concatenate(steps_hi, axis=1), pick) + mm(jnp.concatenate(steps_lo, axis=1), pick)
        return carry

    lax.fori_loop(0, count, chunk, 0)


def backward(proj, bg, mixed, prior, col0, prep, scale, pull, cw, cb, dsk, gain):
    tokens, width = proj.shape[0], proj.shape[1] // 2
    steps = width // CB
    first = col0 // CB
    ins, outs, ins_t, outs_t, meet, run, step = prep

    def whole(shape):
        return pl.BlockSpec(shape, lambda i: (0, 0))

    def cols(rows, base, wide=CB):
        return pl.BlockSpec((rows, wide), lambda i: (0, i + base))

    def heads():
        return pl.BlockSpec((HB, tokens), lambda i: (i + first, 0))

    return pl.pallas_call(
        functools.partial(backward_kernel, col0 // P_SIZE),
        grid=(steps,),
        in_specs=[
            cols(tokens, 0, 2 * CB), cols(tokens, first), cols(tokens, 0), cols(tokens, 0),
            heads(), heads(),
            whole((tokens, NST)), whole((tokens, NST)), whole((NST, tokens)), whole((tokens, Q)),
            whole((tokens, 128)), whole((tokens, 128)),
            cols(CONVK, first), cols(1, first), cols(1, first), cols(1, first),
        ],
        out_specs=[cols(tokens, 0, 2 * CB)] + [whole((tokens, 128))] * 5 + [cols(56, 0)],
        out_shape=(jax.ShapeDtypeStruct((tokens, 2 * width), BF16),)
        + (jax.ShapeDtypeStruct((tokens, 128), F32),) * 5
        + (jax.ShapeDtypeStruct((56, width), F32),),
        scratch_shapes=[pltpu.VMEM((NST, CB), F32), pltpu.VMEM((8, CB), F32)],
        compiler_params=pltpu.CompilerParams(vmem_limit_bytes=56 << 20),
        cost_estimate=pl.CostEstimate(
            flops=int(tokens * width * 12000), bytes_accessed=int(tokens * width * 20), transcendentals=int(tokens * width * 8)
        ),
        name="backward",
    )(proj, bg, mixed, prior, run, step, ins, outs, outs_t, meet, scale, pull, cw, cb, dsk, gain)


def finish_kernel(
    ps_ref, cw_ref, cb_ref, dtb_ref, al_ref, f_ref, ds_ref, dg_ref, dc_ref, db_ref,
    out_ref, vec_ref, ahead,
):
    tri = lower_tri()
    later = (
        lax.broadcasted_iota(jnp.int32, (Q, Q), 0) <= lax.broadcasted_iota(jnp.int32, (Q, Q), 1)
    ).astype(F32)
    vec_ref[...] = jnp.zeros_like(vec_ref)
    ahead[...] = jnp.zeros_like(ahead)
    count = ps_ref.shape[0] // Q

    def chunk(i, carry):
        c = count - 1 - i
        start = pl.multiple_of(c * Q, Q)
        rows = pl.ds(start, Q)
        convs, sigs, pasts, nows = [], [], [], []
        for j in range(2):
            lanes = slice(NST * j, NST * (j + 1))
            now = ps_ref[rows, lanes]
            past = shifted(rows_before(ps_ref, start, lanes), now)
            co = conv_of(now, past, cw_ref[:, lanes], cb_ref[:, lanes])
            convs.append(co)
            sigs.append(jax.nn.sigmoid(co))
            pasts.append(past)
            nows.append(now)
        ins, outs = convs[0] * sigs[0], convs[1] * sigs[1]
        dmeet = jnp.where(tri, dg_ref[rows, :], 0.0)
        dins = mm_exact(dmeet, outs, TN) + db_ref[rows, :]
        douts = mm_exact(dmeet, ins) + dc_ref[rows, :]
        for j, (grad, act) in enumerate(((dins, ins), (douts, outs))):
            lanes = slice(NST * j, NST * (j + 1))
            dco = grad * (sigs[j] + act * (1.0 - sigs[j]))
            for k, source in enumerate((pasts[j][2], pasts[j][1], pasts[j][0], nows[j])):
                vec_ref[8 * k : 8 * k + 8, lanes] += fold8(dco * source)
            vec_ref[32:40, lanes] += fold8(dco)
            spread = jnp.concatenate([dco, ahead[:, lanes]], axis=0)
            ahead[:, lanes] = dco[0:8]
            taps = cw_ref[:, lanes]
            dconv = dco * taps[3:4]
            for k in (1, 2, 3):
                dconv = dconv + pltpu.roll(spread, Q + 8 - k, 0)[:Q] * taps[3 - k : 4 - k]
            out_ref[rows, lanes] = dconv.astype(BF16)
        dt = slice(2 * NST, 3 * NST)
        before = ps_ref[rows, dt] + dtb_ref[...]
        rate = -jnp.exp(al_ref[...])
        ddecay = mm_exact(later, f_ref[rows, :])
        ddt = (ds_ref[rows, :] + rate * ddecay) * jax.nn.sigmoid(before)
        vec_ref[0:8, dt] += fold8(ddt)
        vec_ref[8:16, dt] += fold8(ddecay * rate * jax.nn.softplus(before))
        out_ref[rows, dt] = ddt.astype(BF16)
        return carry

    lax.fori_loop(0, count, chunk, 0)


def finish(ps, cw, cb, dtb, al, f, ds, dg, dc, db):
    tokens = ps.shape[0]
    return pl.pallas_call(
        finish_kernel,
        out_shape=(jax.ShapeDtypeStruct((tokens, 384), BF16), jax.ShapeDtypeStruct((40, 384), F32)),
        scratch_shapes=[pltpu.VMEM((8, 256), F32)],
        compiler_params=pltpu.CompilerParams(vmem_limit_bytes=40 << 20),
        cost_estimate=pl.CostEstimate(flops=800000000, bytes_accessed=int(6e6), transcendentals=1000000),
        name="finish",
    )(ps, cw, cb, dtb, al, f, ds, dg, dc, db)


CHUNKS = ((0, 2), (2, 2), (4, 2), (6, 2), (8, 2))


def rms_norm(tokens_f, gain):
    return tokens_f * lax.rsqrt(jnp.mean(tokens_f * tokens_f, axis=-1, keepdims=True) + EPS) * gain


def chunk_columns(weight, first, steps):
    parts = []
    for s in range(first, first + steps):
        parts.append(weight[:, CB * s : CB * (s + 1)])
        parts.append(weight[:, E + CB * s : E + CB * (s + 1)])
    return jnp.concatenate(parts, axis=1)


def half_rows(weight):
    rows = weight.shape[0] // 2
    return lax.dynamic_slice_in_dim(weight, lax.axis_index("core") * rows, rows, 0)


def gather(half):
    return lax.all_gather(half, ("shard", "core"), axis=0, tiled=True)


def reduce_rows(grad):
    part = lax.psum_scatter(grad, ("shard", "core"), scatter_dimension=0, tiled=True)
    part = lax.psum(part, "far")
    return lax.all_gather(part, "core", axis=0, tiled=True)


def butterfly(value):
    for name in ("core", "shard", "far"):
        size = lax.axis_size(name)
        hop = 1
        while hop < size:
            value = value + lax.ppermute(value, name, [(i, i ^ hop) for i in range(size)])
            hop *= 2
    return value


def body(tokens, w_in, w_dt, w_out, norm_gain, conv_weight, conv_bias, dt_bias, a_log, d_skip, gate_gain, cotangent):
    length = tokens.shape[0]
    tokens_f = tokens.astype(F32)
    half_in = half_rows(w_in)
    side = jnp.concatenate(
        [half_in[:, 2 * E :], half_rows(w_dt), jnp.zeros((half_in.shape[0], 128 - H), BF16)], axis=1
    )
    w_side = gather(side)
    w_out_full = gather(half_rows(w_out))
    w_chunks = [gather(chunk_columns(half_in, first, steps)) for first, steps in CHUNKS]

    normed_f, norm_pull = jax.vjp(rms_norm, tokens_f, norm_gain)
    normed = normed_f.astype(BF16)
    bg = mm(cotangent, w_out_full, NT)

    cw, cb = conv_weight, conv_bias[None]
    cws, cbs = cw[:, E:], cb[:, E:]
    dtb = jnp.pad(dt_bias, (0, 128 - H))[None]
    al = jnp.pad(a_log, (0, 128 - H))[None]
    dsk = jnp.repeat(d_skip, P_SIZE)[None]
    gain = gate_gain[None]

    ps = mm(normed, w_side)
    prep = prepare(ps, cws, cbs, dtb, al)
    projs, fronts = [], []
    for (first, steps), weight in zip(CHUNKS, w_chunks):
        projs.append(mm(normed, weight))
        fronts.append(forward(projs[-1], bg, CB * first, prep, cw, cb, dsk, gain))
    ss = sum(f[3] for f in fronts).sum(axis=1, keepdims=True)
    cg = sum(f[4] for f in fronts).sum(axis=1, keepdims=True)
    r = lax.rsqrt(ss / E + EPS)
    k = r * r * r * cg / E
    scale = jnp.broadcast_to(r, (length, 128))
    pull = jnp.broadcast_to(k, (length, 128))
    y = jnp.concatenate([f[1] for f in fronts], axis=1)
    gated = (y.astype(F32) * r * gain).astype(BF16)
    grad_out = reduce_rows(mm(gated, cotangent, TN).astype(BF16)).astype(F32)
    result = (tokens_f + mm(gated, w_out_full)).astype(BF16)

    totals, vecs, parts = None, [], []
    back = None
    for (first, steps), weight, proj, front in zip(CHUNKS, w_chunks, projs, fronts):
        dproj, *sums, vec = backward(
            proj, bg, front[0], front[2], CB * first, prep, scale, pull, cw, cb, dsk, gain
        )
        totals = sums if totals is None else [a + b for a, b in zip(totals, sums)]
        vecs.append(vec)
        parts.append(reduce_rows(mm(normed, dproj, TN).astype(BF16)))
        term = mm(dproj, weight, NT)
        back = term if back is None else back + term
    dside, svec = finish(ps, cws, cbs, dtb, al, *totals)
    part_side = reduce_rows(mm(normed, dside, TN).astype(BF16))
    back = back + mm(dside, w_side, NT)

    gates, convs = [], []
    for (first, steps), part in zip(CHUNKS, parts):
        for s in range(steps):
            gates.append(part[:, 2 * CB * s : 2 * CB * s + CB])
            convs.append(part[:, 2 * CB * s + CB : 2 * CB * (s + 1)])
    grad_in = jnp.concatenate(gates + convs + [part_side[:, : 2 * NST]], axis=1).astype(F32)
    grad_dt = part_side[:, 2 * NST : 2 * NST + H].astype(F32)

    back_tokens, grad_norm = norm_pull(back)
    token_grad = cotangent.astype(F32) + back_tokens

    vec = jnp.concatenate([v.reshape(7, 8, -1).sum(axis=1) for v in vecs], axis=1)
    svec = svec.reshape(5, 8, -1).sum(axis=1)
    pieces = [
        grad_norm,
        jnp.concatenate([vec[:CONVK], svec[:CONVK, : 2 * NST]], axis=1).reshape(-1),
        jnp.concatenate([vec[CONVK], svec[CONVK, : 2 * NST]]),
        svec[0, 2 * NST : 2 * NST + H],
        svec[1, 2 * NST : 2 * NST + H],
        vec[6].reshape(H, P_SIZE).sum(axis=1),
        vec[5],
    ]
    packed = jnp.concatenate(pieces)
    packed = jnp.pad(packed, (0, -packed.size % 1024)).reshape(-1, 128)
    packed = butterfly(packed).reshape(-1)
    smalls, at = [], 0
    for piece in pieces:
        smalls.append(packed[at : at + piece.size])
        at += piece.size
    return (
        result, token_grad, grad_in, grad_dt, grad_out,
        smalls[0], smalls[1].reshape(CONVK, -1), *smalls[2:],
    )


def solution(mesh):
    replicas, shards = mesh.shape["replica"], mesh.shape["shard"]
    cores = 2 if replicas % 2 == 0 else 1
    inner = Mesh(mesh.devices.reshape(replicas // cores, cores, shards), ("far", "core", "shard"))
    rows = P(("far", "core", "shard"), None)
    held = P("shard", None)
    return jax.shard_map(
        body,
        mesh=inner,
        in_specs=(rows, held, held, held) + (P(),) * 7 + (rows,),
        out_specs=(rows, rows, held, held, held) + (P(),) * 7,
        check_vma=False,
    )
```

time: 2900 us -> 2040 us (0.70)
  matrix products: 853 us -> 404 us
  other arithmetic: 441 us -> 57.4 us
  Pallas kernels: 0 us -> 271 us
  local copies, waits for them, and re-layouts: 311 us -> 77.4 us
  blocking collectives: 52.3 us -> 2.15 us
  waiting for transfers between devices: 1220 us -> 1190 us
    dot_general x21, matrix products: 853 us -> 404 us  [mm(): return lax.dot_general(a, b, dims, preferred_element_type=F32)]
    pallas_call x0 -> x12, Pallas kernels: none -> 271 us  [the longest x5 172 us: backward(): pl.pallas_call(functools.partial(backward_kernel, col0 // P_SIZE), grid=(...]
    reshape x15 -> x3, local copies, waits for them, and re-layouts: 189 us -> 0.72 us  [the longest x1 0.67 us: body(): smalls[1].reshape(CONVK, -1)]
    reduce_sum x7 -> x10, other arithmetic: 140 us -> 4.74 us  [the longest x1 3.9 us: rms_norm(): jnp.mean(tokens_f * tokens_f, axis=-1, keepdims=True) + EPS]
    mul x3 -> x0, other arithmetic: 82.8 us -> none  [the longest x1 48.1 us: mixer(): activ = jax.nn.silu(conv_out)]
    all_gather x2 -> x13, waiting for transfers between devices: 439 us -> 366 us  [the longest x7 366 us: gather(): return lax.all_gather(half, ('shard', 'core'), axis=0, tiled=True)]
    add_any x3 -> x0, other arithmetic: 54.6 us -> none  [the longest x2 36.8 us: mixer(): conv_out = conv_bias + padded[0:length] * conv_weight[0]]
    slice x8 -> x14, local copies, waits for them, and re-layouts: 55.8 us -> 9.65 us  [the longest x1 4.3 us: chunk_columns(): parts.append(weight[:, CB * s:CB * (s + 1)])]
  transfers between devices with their start and end apart: 7 -> 26, of which waited for: 4 -> 16; matrix products, arithmetic and copies ran while one was open for 37% -> 23% of each run, Pallas kernels for 0% -> 0%
where the time goes in v1:
time: 2040 us; the launch traced here: 2020 us
  waiting for transfers between devices  1190 us (58%)
  matrix products  404 us (20%)
  Pallas kernels  271 us (13%)
  local copies, waits for them, and re-layouts  77.4 us (4%)
  other arithmetic  57.4 us (3%)
    reduce_scatter x7, waiting for transfers between devices, reduce_rows(): lax.psum_scatter(grad, ('shard', 'core'), scatter_dimension=0, tiled=True)  495 us
    dot_general x21, matrix products, mm(): return lax.dot_general(a, b, dims, preferred_element_type=F32)  404 us
    all_gather x7, waiting for transfers between devices, gather(): return lax.all_gather(half, ('shard', 'core'), axis=0, tiled=True)  366 us
    psum x1, waiting for transfers between devices, reduce_rows(): part = lax.psum(part, 'far')  316 us
    pallas_call x5, Pallas kernels, backward(): pl.pallas_call(functools.partial(backward_kernel, col0 // P_SIZE), grid=(...  172 us
    pallas_call x5, Pallas kernels, forward(): pl.pallas_call(forward_kernel, grid=(steps,), in_specs=[cols(tokens, 0, 2...  91.4 us
    unnamed x193, local copies, waits for them, and re-layouts  58.3 us
  transfers between devices with their start and end apart: 26, of which 16 were waited for; matrix products, arithmetic and copies ran while one was open for 23% of the time, Pallas kernels for 0%

profile of v1, /device:TPU:8, one launch (start us, length us, event | category | flops | bytes accessed | tf_op | source)
XLA Modules:
  0.0 2023.4 jit_solution(16618394688536061995)
XLA Ops:
  50.9 53.7 %all-gather.20.cloned.1.call-done = bf16[2560,2048]{1,0:T(8,128)(2,1)} async-done(((bf16[320,2048]{1,0:T(8,128)(2,1)}), bf16[2560,2048]{1,0:T(8,128)(2,1)}) %all-gather.20.cloned.1.call-update) | async-done | bytes 10485776 | tf_op jit(solution)/shard_map/all_gather | solution.py:486
  121.9 48.4 %all-gather.22.cloned.1.call-done = bf16[2560,2048]{1,0:T(8,128)(2,1)} async-done(((bf16[320,2048]{1,0:T(8,128)(2,1)}), bf16[2560,2048]{1,0:T(8,128)(2,1)}) %all-gather.22.cloned.1.call-update) | async-done | bytes 10485776 | tf_op jit(solution)/shard_map/all_gather | solution.py:486
  187.6 47.7 %all-gather.24.cloned.1.call-done = bf16[2560,2048]{1,0:T(8,128)(2,1)} async-done(((bf16[320,2048]{1,0:T(8,128)(2,1)}), bf16[2560,2048]{1,0:T(8,128)(2,1)}) %all-gather.24.cloned.1.call-update) | async-done | bytes 10485776 | tf_op jit(solution)/shard_map/all_gather | solution.py:486
  253.0 48.0 %all-gather.14.cloned.1.call-done = bf16[2560,2048]{1,0:T(8,128)(2,1)} async-done(((bf16[320,2048]{1,0:T(8,128)(2,1)}), bf16[2560,2048]{1,0:T(8,128)(2,1)}) %all-gather.14.cloned.1.call-update) | async-done | bytes 10485776 | tf_op jit(solution)/shard_map/all_gather | solution.py:486
  318.3 47.7 %all-gather.26.cloned.1.call-done = bf16[2560,2048]{1,0:T(8,128)(2,1)} async-done(((bf16[320,2048]{1,0:T(8,128)(2,1)}), bf16[2560,2048]{1,0:T(8,128)(2,1)}) %all-gather.26.cloned.1.call-update) | async-done | bytes 10485776 | tf_op jit(solution)/shard_map/all_gather | solution.py:486
  383.3 114.9 %all-gather.16.cloned.1.call-done = bf16[5120,2560]{1,0:T(8,128)(2,1)} async-done(((bf16[640,2560]{1,0:T(8,128)(2,1)}), bf16[5120,2560]{1,0:T(8,128)(2,1)}) %all-gather.16.cloned.1.call-update) | async-done | bytes 26214416 | tf_op jit(solution)/shard_map/all_gather | solution.py:486
  498.2 34.3 %convolution_bitcast_fusion.bg_ref = f32[1024,5120]{1,0:T(8,128)} fusion(bf16[5120,2560]{1,0:T(8,128)(2,1)} %all-gather.16.cloned.1.call-done, bf16[1024,2560]{1,0:T(8,128)(2,1)} %param.23), kind=kOutput, calls=%fused_computation.15 | convolution fusion | flops 26843545600 | bytes 52428800 | tf_op jit(solution)/shard_map/dot_general | solution.py:29
  532.5 18.3 forward.9
  591.2 18.3 forward.6
  632.5 34.4 %backward.9 = (bf16[1024,2048]{1,0:T(8,128)(2,1)}, f32[1024,128]{1,0:T(8,128)}, f32[1024,128]{1,0:T(8,128)}, f32[1024,128]{1,0:T(8,128)}, f32[1024,128]{1,0:T(8,...) custom-call(f32[1024,2048]{1,0:T(8,128)} %fusion.18.both_ref, f32[1024,5120]{1,0:T(8,128)} %convolution_bitcast_fusion.bg_ref, ...), custom_call_target="tpu_custom_call" | custom-call | flops 12582912000 | bytes 20971520 | tf_op jit(solution)/shard_map/backward/pallas_call | solution.py:374
  666.9 34.4 %backward.8 = (bf16[1024,2048]{1,0:T(8,128)(2,1)}, f32[1024,128]{1,0:T(8,128)}, f32[1024,128]{1,0:T(8,128)}, f32[1024,128]{1,0:T(8,128)}, f32[1024,128]{1,0:T(8,...) custom-call(f32[1024,2048]{1,0:T(8,128)} %fusion.20.both_ref, f32[1024,5120]{1,0:T(8,128)} %convolution_bitcast_fusion.bg_ref, ...), custom_call_target="tpu_custom_call" | custom-call | flops 12582912000 | bytes 20971520 | tf_op jit(solution)/shard_map/backward/pallas_call | solution.py:374
  701.4 34.7 %backward.7 = (bf16[1024,2048]{1,0:T(8,128)(2,1)}, f32[1024,128]{1,0:T(8,128)}, f32[1024,128]{1,0:T(8,128)}, f32[1024,128]{1,0:T(8,128)}, f32[1024,128]{1,0:T(8,...) custom-call(f32[1024,2048]{1,0:T(8,128)} %fusion.22.both_ref, f32[1024,5120]{1,0:T(8,128)} %convolution_bitcast_fusion.bg_ref, ...), custom_call_target="tpu_custom_call" | custom-call | flops 12582912000 | bytes 20971520 | tf_op jit(solution)/shard_map/backward/pallas_call | solution.py:374
  736.1 34.4 %backward.6 = (bf16[1024,2048]{1,0:T(8,128)(2,1)}, f32[1024,128]{1,0:T(8,128)}, f32[1024,128]{1,0:T(8,128)}, f32[1024,128]{1,0:T(8,128)}, f32[1024,128]{1,0:T(8,...) custom-call(f32[1024,2048]{1,0:T(8,128)} %fusion.24.both_ref, f32[1024,5120]{1,0:T(8,128)} %convolution_bitcast_fusion.bg_ref, ...), custom_call_target="tpu_custom_call" | custom-call | flops 12582912000 | bytes 20971520 | tf_op jit(solution)/shard_map/backward/pallas_call | solution.py:374
  770.6 34.5 %backward.5 = (bf16[1024,2048]{1,0:T(8,128)(2,1)}, f32[1024,128]{1,0:T(8,128)}, f32[1024,128]{1,0:T(8,128)}, f32[1024,128]{1,0:T(8,128)}, f32[1024,128]{1,0:T(8,...) custom-call(f32[1024,2048]{1,0:T(8,128)} %fusion.28.both_ref, f32[1024,5120]{1,0:T(8,128)} %convolution_bitcast_fusion.bg_ref, ...), custom_call_target="tpu_custom_call" | custom-call | flops 12582912000 | bytes 20971520 | tf_op jit(solution)/shard_map/backward/pallas_call | solution.py:374
  873.0 18.7 convolution_convert_fusion.2
  923.0 37.9 %convolution_convert_fusion = bf16[5120,2560]{1,0:T(8,128)(2,1)} fusion(bf16[1024,2560]{1,0:T(8,128)(2,1)S(1)} %bitcast.78, bf16[1024,5120]{1,0:T(8,128)(2,1)} %constant_dynamic-update-slice_fusion, f32[5120]{0:T(1024)S(1)} %copy-done.15, f32[1024]{0:T(1024)S(1)} %copy-done.73), kind=kOutput, calls=%fused_computation | convolution fusion | flops 26877624320 | bytes 41967616 | tf_op jit(solution)/shard_map/dot_general | solution.py:29
  961.0 71.4 %reduce-scatter.10.cloned.1.call-done = bf16[320,2048]{1,0:T(8,128)(2,1)} async-done(((bf16[2560,2048]{1,0:T(8,128)(2,1)}), bf16[320,2048]{1,0:T(8,128)(2,1)}) %reduce-scatter.10.cloned.1.call-update) | async-done | bytes 1310736 | tf_op jit(solution)/shard_map/reduce_scatter | solution.py:490
  1032.4 85.5 %reduce-scatter.12.cloned.1.call-done = bf16[320,2048]{1,0:T(8,128)(2,1)} async-done(((bf16[2560,2048]{1,0:T(8,128)(2,1)}), bf16[320,2048]{1,0:T(8,128)(2,1)}) %reduce-scatter.12.cloned.1.call-update) | async-done | bytes 1310736 | tf_op jit(solution)/shard_map/reduce_scatter | solution.py:490
  1117.9 85.4 %reduce-scatter.14.cloned.1.call-done = bf16[320,2048]{1,0:T(8,128)(2,1)} async-done(((bf16[2560,2048]{1,0:T(8,128)(2,1)}), bf16[320,2048]{1,0:T(8,128)(2,1)}) %reduce-scatter.14.cloned.1.call-update) | async-done | bytes 1310736 | tf_op jit(solution)/shard_map/reduce_scatter | solution.py:490
  1203.3 85.5 %reduce-scatter.16.cloned.1.call-done = bf16[320,2048]{1,0:T(8,128)(2,1)} async-done(((bf16[2560,2048]{1,0:T(8,128)(2,1)}), bf16[320,2048]{1,0:T(8,128)(2,1)}) %reduce-scatter.16.cloned.1.call-update) | async-done | bytes 1310736 | tf_op jit(solution)/shard_map/reduce_scatter | solution.py:490
  1288.8 167.0 %reduce-scatter.20.cloned.1.call-done = bf16[640,2560]{1,0:T(8,128)(2,1)} async-done(((bf16[5120,2560]{1,0:T(8,128)(2,1)}), bf16[640,2560]{1,0:T(8,128)(2,1)}) %reduce-scatter.20.cloned.1.call-update) | async-done | bytes 3276816 | tf_op jit(solution)/shard_map/reduce_scatter | solution.py:490
  1490.5 316.2 %all-reduce.6.cloned.1.call-done = (bf16[320,2048]{1,0:T(8,128)(2,1)}, bf16[320,2048]{1,0:T(8,128)(2,1)}, bf16[320,2048]{1,0:T(8,128)(2,1)}, bf16[320,2048]{1,0:...) async-done(((bf16[320,2048]{1,0:T(8,128)(2,1)}, bf16[320,2048]{1,0:T(8,128)(2,1)}, bf16[320,2048]{1,0:T(8,128)(2,1)}, ...) | async-done | bytes 10076176 | tf_op jit(solution)/shard_map/psum | solution.py:491
  1859.9 24.6 %fusion.3 = (f32[2560]{0:T(1024)S(1)}, f32[1024]{0:T(1024)S(1)}, f32[1024,2560]{1,0:T(8,128)}) fusion(bf16[1024,2560]{1,0:T(8,128)(2,1)} %param.12, f32[1024]{0:T(1024)S(1)} %copy-done.70, f32[2560]{0:T(1024)S(1)} %copy-done.65, bf16[1024,384]{1,0:T(8,128)(2,1)S(1)} %copy-done.10, bf16[2560,384]{1,0:T(8,128)(2,1)S(1)} %copy-done.36, ...), kind=kOutput, calls=%fused_computation.17 | convolution fusion | flops 2044719616 | bytes 70938624 | tf_op jit(solution)/shard_map/dot_general | solution.py:29
  1893.8 35.3 %fusion.6 = bf16[1024,2560]{1,0:T(8,128)(2,1)} fusion(bf16[1024,2560]{1,0:T(8,128)(2,1)} %param.12, bf16[5120,2560]{1,0:T(8,128)(2,1)} %all-gather.16.cloned.1.call-done, bf16[1024,5120]{1,0:T(8,128)(2,1)} %constant_dynamic-update-slice_fusion, f32[5120]{0:T(1024)S(1)} %copy-done.15, f32[1024]{0:T(1024)S(1)} %copy-done.73), kind=kOutput, calls=%fused_computation.20 | convolution fusion | flops 26872381440 | bytes 47210496 | tf_op jit(solution)/shard_map/dot_general | solution.py:29
  (346 shorter events, 476.3 us)
Async XLA Ops:
  7.2 31.6 %all-gather.18.cloned.1.call-start = ((), (), s32[]{:S(2)}) async-start(), calls=%async_computation.9 | async-start | bytes 2211840 | tf_op jit(solution)/shard_map/all_gather | solution.py:486
  10.1 94.4 %all-gather.20.cloned.1.call-start = ((), (), s32[]{:S(2)}) async-start(), calls=%async_computation.10 | async-start | bytes 11796480 | tf_op jit(solution)/shard_map/all_gather | solution.py:486
  15.7 154.6 %all-gather.22.cloned.1.call-start = ((), (), s32[]{:S(2)}) async-start(), calls=%async_computation.11 | async-start | bytes 11796480 | tf_op jit(solution)/shard_map/all_gather | solution.py:486
  18.3 217.0 %all-gather.24.cloned.1.call-start = ((), (), s32[]{:S(2)}) async-start(), calls=%async_computation.12 | async-start | bytes 11796480 | tf_op jit(solution)/shard_map/all_gather | solution.py:486
  19.7 281.3 %all-gather.14.cloned.1.call-start = ((), (), s32[]{:S(2)}) async-start(), calls=%async_computation.7 | async-start | bytes 11796480 | tf_op jit(solution)/shard_map/all_gather | solution.py:486
  22.1 343.8 %all-gather.26.cloned.1.call-start = ((), (), s32[]{:S(2)}) async-start(), calls=%async_computation.13 | async-start | bytes 11796480 | tf_op jit(solution)/shard_map/all_gather | solution.py:486
  23.4 474.8 %all-gather.16.cloned.1.call-start = ((), (), s32[]{:S(2)}) async-start(), calls=%async_computation.8 | async-start | bytes 29491200 | tf_op jit(solution)/shard_map/all_gather | solution.py:486
  27.3 933.7 %reduce-scatter.18.cloned.1.call-start = ((), (), s32[]{:S(2)}) async-start(), calls=%async_computation.24 | async-start | bytes 2211840 | tf_op jit(solution)/shard_map/reduce_scatter | solution.py:490
  820.5 140.5 %reduce-scatter.8.cloned.1.call-start = ((), (), s32[]{:S(2)}) async-start(), calls=%async_computation.14 | async-start | bytes 11796480 | tf_op jit(solution)/shard_map/reduce_scatter | solution.py:490
  838.1 194.3 %reduce-scatter.10.cloned.1.call-start = ((), (), s32[]{:S(2)}) async-start(), calls=%async_computation.16 | async-start | bytes 11796480 | tf_op jit(solution)/shard_map/reduce_scatter | solution.py:490
  855.3 262.6 %reduce-scatter.12.cloned.1.call-start = ((), (), s32[]{:S(2)}) async-start(), calls=%async_computation.18 | async-start | bytes 11796480 | tf_op jit(solution)/shard_map/reduce_scatter | solution.py:490
  873.0 330.3 %reduce-scatter.14.cloned.1.call-start = ((), (), s32[]{:S(2)}) async-start(), calls=%async_computation.20 | async-start | bytes 11796480 | tf_op jit(solution)/shard_map/reduce_scatter | solution.py:490
  891.8 397.0 %reduce-scatter.16.cloned.1.call-start = ((), (), s32[]{:S(2)}) async-start(), calls=%async_computation.22 | async-start | bytes 11796480 | tf_op jit(solution)/shard_map/reduce_scatter | solution.py:490
  909.6 546.1 %reduce-scatter.20.cloned.1.call-start = ((), (), s32[]{:S(2)}) async-start(), calls=%async_computation.25 | async-start | bytes 29491200 | tf_op jit(solution)/shard_map/reduce_scatter | solution.py:490
  960.9 845.7 %all-reduce.6.cloned.1.call-start = ((), (), s32[]{:S(2)}) async-start(), calls=%async_computation.27 | async-start | bytes 20152320 | tf_op jit(solution)/shard_map/psum | solution.py:491
  1455.8 501.0 %all-gather.28.cloned.1.call-start = ((), (), s32[]{:S(2)}) async-start(), calls=%async_computation.15 | async-start | bytes 3932160 | tf_op jit(solution)/shard_map/all_gather | solution.py:492
  1806.7 154.2 %all-gather.30.cloned.1.call-start = ((), (), s32[]{:S(2)}) async-start(), calls=%async_computation.17 | async-start | bytes 3932160 | tf_op jit(solution)/shard_map/all_gather | solution.py:492
  1824.3 140.6 %all-gather.32.cloned.1.call-start = ((), (), s32[]{:S(2)}) async-start(), calls=%async_computation.19 | async-start | bytes 3932160 | tf_op jit(solution)/shard_map/all_gather | solution.py:492
  1841.8 127.2 %all-gather.34.cloned.1.call-start = ((), (), s32[]{:S(2)}) async-start(), calls=%async_computation.21 | async-start | bytes 3932160 | tf_op jit(solution)/shard_map/all_gather | solution.py:492
  1859.8 113.2 %all-gather.36.cloned.1.call-start = ((), (), s32[]{:S(2)}) async-start(), calls=%async_computation.23 | async-start | bytes 3932160 | tf_op jit(solution)/shard_map/all_gather | solution.py:492
  1891.9 37.1 %collective-permute-start.2 = (f32[272,128]{1,0:T(8,128)S(1)}, f32[272,128]{1,0:T(8,128)S(1)}, u32[]{:S(2)}, u32[]{:S(2)}) collective-permute-start(f32[272,128]{1,0:T(8,128)S(1)} %fusion.67), channel_id=1, source_target_pairs={{0,2},{1,3},{2,0},{3,1},{4,6},{5,7},{6,4},{7,5},{8,10},{9,11},{10,... | collective-permute-start | bytes 417800 | tf_op jit(solution)/shard_map/ppermute | solution.py:500
  1893.7 112.8 %all-gather.38.cloned.1.call-start = ((), (), s32[]{:S(2)}) async-start(), calls=%async_computation.26 | async-start | bytes 9830400 | tf_op jit(solution)/shard_map/all_gather | solution.py:492
  1929.1 6.6 collective-permute-start.3
  1935.7 14.8 collective-permute-start.4
  (84 other events, 7282.9 us)
Sparse Core Ops, SparseCore 0:
  10.2 28.4 all-gather.17
  41.2 63.2 all-gather.19
  107.0 63.2 all-gather.21
  172.0 63.2 all-gather.23
  237.6 63.2 all-gather.13
  302.7 63.2 all-gather.25
  368.4 129.7 all-gather.15
  820.6 40.2 reduce-scatter.17
  865.5 81.5 reduce-scatter.7
  950.8 81.5 reduce-scatter.9
  1036.3 81.5 reduce-scatter.11
  1121.7 81.5 reduce-scatter.13
  1207.2 81.5 reduce-scatter.15
  1293.4 162.3 reduce-scatter.19
  1459.5 347.1 all-reduce.5
  1808.1 12.6 all-gather.27
  1824.4 12.6 all-gather.29
  1841.9 12.6 all-gather.31
  1860.0 12.6 all-gather.33
  1893.8 11.5 all-gather.35
  1936.8 17.5 all-gather.37
